TPU v7x, 32 devices: a whole 2x2x4 slice. The times are simulated.
32 devices in a mesh: ind: 4 (over x, core), mark: 4 (over z), chip: 2 (over y).
Axes of the slice: x: 2, y: 2, z: 4, core: 2. Of those that a mesh axis runs over, the one named last changes fastest.
Arguments:
- genotypes: bfloat16 [8192, 8192], P(('ind', 'chip'), 'mark'), may hold values from -0.1875 to 0.1875
- residual: float32 [8192, 1024], P(('ind', 'chip'), 'mark'), as said below
- posterior_inverse: bfloat16 [8, 1024, 1024], P('mark'), as said below
- gibbs_noise: bfloat16 [4, 8192, 256], P(None, 'mark'), may hold values from -6 to 6
- visit_order: int32 [4, 4, 2], P(None, 'mark'), may hold values from 0 to 1, each once within a row
Outputs:
- residual_after: float32 [8192, 1024], P(('ind', 'chip'), 'mark')
- effect_changes: float32 [4, 8192, 256], P(None, 'mark')
Inputs may be any that keep to these rules, and one draw needn't show every extreme that they name: `visit_order`: each row names each of the 2 marker blocks of one cycle position once. `residual`: finite real values. `posterior_inverse`: the diagonal entries are positive.
All inputs are finite; a program needn't handle non-finite values.
Results may differ from a plain program's by a relative error of at most 0.005.
Values sent between devices are 32-bit elements; how exact they have to be, the bound alone decides.
A program may use at most 128 MiB of HBM per device.

v0:
```python
import functools

import jax
import jax.numpy as jnp
from jax import lax
from jax.experimental import pallas as pl
from jax.experimental.pallas import tpu as pltpu
from jax.sharding import PartitionSpec as P

epsilon = 1e-05
MESH = pl.DeviceIdType.MESH
CHUNKS = 4
PERIOD = 6
ORDER = (
    ("m", 3),
    ("c", 4),
    ("l", 5),
    ("d", 2),
    ("b", 3),
    ("a", 0),
    ("c", 1),
    ("d", 4),
    ("b", 0),
)
NT = (((1,), (1,)), ((), ()))


def kernel(
    cfg,
    order_ref,
    geno_hbm,
    resid_hbm,
    inv_hbm,
    noise_hbm,
    after_hbm,
    change_hbm,
    geno_ref,
    resid_ref,
    inv_ref,
    noise_raw,
    noise_ref,
    droot_ref,
    change_ref,
    ebuf,
    part,
    r1,
    r2,
    full,
    scaled,
    stash,
    in_sem,
    out_sem,
    after_sem,
    p1s,
    p1r,
    p2s,
    p2r,
    p3s,
    p3r,
    p4s,
    zs,
    zr,
):
    n_ind, n_mark, n_chip, chunks, stops, count, block, rows, lanes, sq_rows = cfg
    quads = n_ind // 2 * n_chip
    tc = ebuf.shape[2]
    lane_blocks = block // lanes
    sq_groups = tc // sq_rows
    ind = lax.axis_index("ind")
    mark = lax.axis_index("mark")
    y = lax.axis_index("chip")
    core = lax.rem(ind, 2)
    other = 1 - core
    q = lax.div(ind, 2) * n_chip + y
    partner = {"ind": ind + 1 - 2 * core}
    nxt = {"mark": lax.rem(mark + 1, n_mark)}
    prv = {"mark": lax.rem(mark + n_mark - 1, n_mark)}

    x_chips = n_ind // 2
    steps = [(dx, dy) for dx in range(x_chips) for dy in range(n_chip)][1:]
    steps.sort(key=lambda d: min(d[0], x_chips - d[0]) + min(d[1], n_chip - d[1]))

    def chip_at(r):
        xx = lax.rem(lax.div(ind, 2) + steps[r - 1][0], x_chips)
        yy = lax.rem(y + steps[r - 1][1], n_chip)
        return xx * n_chip + yy, {"ind": xx * 2 + core, "chip": yy}

    blocks = geno_ref.shape[0]
    per_visit = chunks // blocks
    piece = noise_ref.shape[3]
    loads = [pltpu.make_async_copy(resid_hbm, resid_ref, in_sem.at[0])]
    for k in range(blocks):
        loads.append(
            pltpu.make_async_copy(
                geno_hbm.at[:, k * block : (k + 1) * block], geno_ref.at[k], in_sem.at[1 + k]
            )
        )
    loads.append(pltpu.make_async_copy(noise_hbm, noise_raw, in_sem.at[1 + blocks]))
    loads.append(pltpu.make_async_copy(inv_hbm, inv_ref, in_sem.at[2 + blocks]))
    for load in loads:
        load.start()

    barrier = pltpu.get_barrier_semaphore()
    pl.semaphore_signal(barrier, inc=1, device_id=partner, device_id_type=MESH)
    pl.semaphore_signal(barrier, inc=1, device_id=nxt, device_id_type=MESH)
    pl.semaphore_signal(barrier, inc=1, device_id=prv, device_id_type=MESH)
    for r in range(1, quads):
        pl.semaphore_signal(barrier, inc=1, device_id=chip_at(r)[1], device_id_type=MESH)

    loads[0].wait()
    flipped = resid_ref[...].T
    for c in range(chunks):
        ebuf[0, c] = flipped[c * tc : (c + 1) * tc]
    for k in range(blocks):
        loads[1 + k].wait()
    pl.semaphore_wait(barrier, quads + 2)

    def copy(src, dst, ssem, rsem, dev):
        return pltpu.make_async_remote_copy(
            src_ref=src, dst_ref=dst, send_sem=ssem, recv_sem=rsem, device_id=dev, device_id_type=MESH
        )

    def hop(stop, c):
        return copy(ebuf.at[stop, c], ebuf.at[stop + 1, c], zs.at[stop, c], zr.at[stop, c], nxt)

    def pair(c):
        return copy(part.at[c, other], r1.at[c], p1s.at[c], p1r.at[c], partner)

    def spread_out(c, r):
        qq, dev = chip_at(r)
        return copy(part.at[c, core, qq], r2.at[c, q], p2s.at[c, qq], p2r.at[c, q], dev)

    def arrived2(c, r):
        qq, dev = chip_at(r)
        return copy(part.at[c, core, qq], r2.at[c, qq], p2s.at[c, qq], p2r.at[c, qq], dev)

    def gather(c, r):
        qq, dev = chip_at(r)
        return copy(full.at[c, core, q], full.at[c, core, q], p3s.at[c, qq], p3r.at[c, core, q], dev)

    def arrived3(c, r):
        qq, dev = chip_at(r)
        return copy(full.at[c, core, qq], full.at[c, core, qq], p3s.at[c, qq], p3r.at[c, core, qq], dev)

    def forward(c, qq):
        return copy(full.at[c, core, qq], full.at[c, core, qq], p4s.at[c, qq], p3r.at[c, core, qq], partner)

    def arrived4(c, qq):
        return copy(full.at[c, other, qq], full.at[c, other, qq], p4s.at[c, qq], p3r.at[c, other, qq], partner)

    def score(stop, j, c):
        k = order_ref[stop, 0, j]
        e = ebuf[stop, c]
        s = jnp.dot(e.astype(jnp.bfloat16), geno_ref[k], preferred_element_type=jnp.float32)
        sq = e * e
        width = sq.shape[1] // lanes
        tot = sq[:, :lanes]
        for i in range(1, width):
            tot = tot + sq[:, i * lanes : (i + 1) * lanes]
        for d in range(2 * quads):
            rg, lb = d // lane_blocks, d % lane_blocks
            sg = d % sq_groups
            part[c, d // quads, d % quads, :rows, :] = s[
                rg * rows : (rg + 1) * rows, lb * lanes : (lb + 1) * lanes
            ]
            part[c, d // quads, d % quads, rows:, :] = tot[sg * sq_rows : (sg + 1) * sq_rows]
        pair(c).start()

    def phase_a(stop, c):
        @pl.when(stop > 0)
        def _():
            hop(stop - 1, c).wait()

        score(stop, 0, c)

    def phase_b(stop, c):
        pair(c).wait()
        part[c, core] = part[c, core] + r1[c]
        for r in reversed(range(1, quads)):
            spread_out(c, r).start()

    def phase_c(stop, c):
        tot = part[c, core, q]
        for r in range(1, quads):
            arrived2(c, r).wait_recv()
            tot = tot + r2[c, chip_at(r)[0]]
        full[c, core, q] = tot
        for r in reversed(range(1, quads)):
            gather(c, r).start()
        forward(c, q).start()
        for r in range(1, quads):
            spread_out(c, r).wait_send()

    def phase_d(stop, c):
        for r in range(1, quads):
            arrived3(c, r).wait_recv()
            forward(c, chip_at(r)[0]).start()
        for r in range(1, quads):
            gather(c, r).wait_send()

    def phase_e(stop, j, c):
        for r in range(quads):
            arrived4(c, r).wait_recv()
            forward(c, r).wait_send()
        k = order_ref[stop, 0, j]
        for d in range(2 * quads):
            rg, lb = d // lane_blocks, d % lane_blocks
            scaled[rg * rows : (rg + 1) * rows, lb * lanes : (lb + 1) * lanes] = (
                full[c, d // quads, d % quads, :rows, :] * (1.0 / count)
            ).astype(jnp.bfloat16)
        sq = jnp.concatenate(
            [full[c, g // quads, g % quads, rows:, :] for g in range(sq_groups)], axis=0
        )
        spread = jnp.sum(sq, axis=1, keepdims=True) * (1.0 / count)
        root = jnp.sqrt((spread + epsilon) * (1.0 / count))
        mean = lax.dot_general(scaled[...], inv_ref[k], NT, preferred_element_type=jnp.float32)
        noise = jnp.concatenate(
            [
                noise_ref[stop, j * per_visit + i, pl.ds(pl.multiple_of(c * tc, tc), tc), :]
                for i in range(per_visit)
            ],
            axis=1,
        ).astype(jnp.float32)
        change = mean + (root * droot_ref[k]) * noise
        if j == 0:
            stash[c, 0] = change
        else:
            stash[c, 1] = change
            first = order_ref[stop, 0, 0]
            change_ref[stop, 0, c] = stash[c, first]
            change_ref[stop, 1, c] = stash[c, 1 - first]
        ebuf[stop, c] = ebuf[stop, c] - lax.dot_general(
            change.astype(jnp.bfloat16), geno_ref[k], NT, preferred_element_type=jnp.float32
        )

    def at(x, fn):
        stop, c = lax.div(x, PERIOD), lax.rem(x, PERIOD)

        @pl.when((x >= 0) & (c < chunks) & (stop < stops))
        def _():
            fn(stop, c)

    def out_copy(stop, c):
        return pltpu.make_async_copy(change_ref.at[stop, :, c], change_hbm.at[stop, :, c], out_sem.at[stop, c])

    def last(stop, c):
        phase_e(stop, 1, c)
        hop(stop, c).start()
        out_copy(stop, c).start()

    def flip(stop, i):
        noise_ref[stop, i] = noise_raw[stop, pl.ds(pl.multiple_of(i * piece, piece), piece), :].T

    def prepare():
        loads[1 + blocks].wait()
        lax.fori_loop(0, chunks, lambda i, x: (flip(0, i), x)[1], 0)
        loads[2 + blocks].wait()
        eye = lax.broadcasted_iota(jnp.int32, (128, 128), 0) == lax.broadcasted_iota(
            jnp.int32, (128, 128), 1
        )
        for k in range(blocks):
            for i in range(0, block, 128):
                tile = inv_ref[k, i : i + 128, i : i + 128].astype(jnp.float32)
                diag = jnp.sum(jnp.where(eye, tile, 0.0), axis=0, keepdims=True)
                droot_ref[k, :, i : i + 128] = jnp.sqrt(diag)

    def middle(stop, c):
        phase_e(stop, 0, c)
        score(stop, 1, c)

    phases = {
        "a": phase_a,
        "b": phase_b,
        "c": phase_c,
        "d": phase_d,
        "m": middle,
        "l": last,
    }

    def body(t, carry):
        for name, delay in ORDER:
            if name == "b" and delay == 0:
                pl.when(t == 0)(prepare)
            at(t - delay, phases[name])
        at(t + PERIOD, flip)
        return carry

    lax.fori_loop(0, PERIOD * (stops - 1) + chunks + max(delay for _, delay in ORDER), body, 0)
    def finish(c):
        return pltpu.make_async_copy(ebuf.at[stops, c], after_hbm.at[c], after_sem.at[c])

    for c in range(chunks):
        hop(stops - 1, c).wait()
        finish(c).start()
    for c in range(chunks):
        for stop in range(stops):
            out_copy(stop, c).wait()
        finish(c).wait()


def local(mesh_shape, genotypes, residual, posterior_inverse, gibbs_noise, visit_order):
    n_ind, n_mark, n_chip = mesh_shape
    quads = n_ind // 2 * n_chip
    people, traits = residual.shape
    count = people * n_ind * n_chip
    blocks, block = posterior_inverse.shape[:2]
    stops = gibbs_noise.shape[0]
    chunks = CHUNKS
    tc = traits // chunks
    slices = 2 * quads
    lanes = block // min(slices, block // 128)
    rows = tc * (block // lanes) // slices
    sq_rows = max(8, tc // slices)
    f32 = jnp.float32
    cfg = (n_ind, n_mark, n_chip, chunks, stops, count, block, rows, lanes, sq_rows)
    hbm = pl.BlockSpec(memory_space=pl.ANY)
    dma = pltpu.SemaphoreType.DMA
    after, changes = pl.pallas_call(
        functools.partial(kernel, cfg),
        out_shape=(
            jax.ShapeDtypeStruct((chunks, tc, people), f32),
            jax.ShapeDtypeStruct((stops, blocks, chunks, tc, block), f32),
        ),
        in_specs=[pl.BlockSpec(memory_space=pltpu.SMEM)] + [hbm] * 4,
        out_specs=(hbm, hbm),
        scratch_shapes=[
            pltpu.VMEM((blocks, people, block), jnp.bfloat16),
            pltpu.VMEM((people, traits), f32),
            pltpu.VMEM((blocks, block, block), jnp.bfloat16),
            pltpu.VMEM((stops, blocks * block, traits), jnp.bfloat16),
            pltpu.VMEM((stops, chunks, traits, blocks * block // chunks), jnp.bfloat16),
            pltpu.VMEM((blocks, 1, block), f32),
            pltpu.VMEM((stops, blocks, chunks, tc, block), f32),
            pltpu.VMEM((stops + 1, chunks, tc, people), f32),
            pltpu.VMEM((chunks, 2, quads, rows + sq_rows, lanes), f32),
            pltpu.VMEM((chunks, quads, rows + sq_rows, lanes), f32),
            pltpu.VMEM((chunks, quads, rows + sq_rows, lanes), f32),
            pltpu.VMEM((chunks, 2, quads, rows + sq_rows, lanes), f32),
            pltpu.VMEM((tc, block), jnp.bfloat16),
            pltpu.VMEM((chunks, blocks, tc, block), f32),
            dma((3 + blocks,)),
            dma((stops, chunks)),
            dma((chunks,)),
            dma((chunks,)),
            dma((chunks,)),
            dma((chunks, quads)),
            dma((chunks, quads)),
            dma((chunks, quads)),
            dma((chunks, 2, quads)),
            dma((chunks, quads)),
            dma((stops, chunks)),
            dma((stops, chunks)),
        ],
        compiler_params=pltpu.CompilerParams(
            collective_id=0, has_side_effects=True, vmem_limit_bytes=56 * 1024 * 1024
        ),
    )(visit_order, genotypes, residual, posterior_inverse, gibbs_noise)
    after = after.reshape(traits, people).T
    changes = changes.reshape(stops, blocks, traits, block).transpose(0, 1, 3, 2)
    return after, changes.reshape(stops, blocks * block, traits)


def solution(mesh):
    in_specs = (
        P(("ind", "chip"), "mark"),
        P(("ind", "chip"), "mark"),
        P("mark", None, None),
        P(None, "mark", None),
        P(None, "mark", None),
    )
    out_specs = (P(("ind", "chip"), "mark"), P(None, "mark", None))
    shape = (mesh.shape["ind"], mesh.shape["mark"], mesh.shape["chip"])
    return jax.shard_map(
        functools.partial(local, shape), mesh=mesh, in_specs=in_specs, out_specs=out_specs, check_vma=False
    )
```

profile of v0, /device:TPU:0, one launch (start us, length us, event | category | flops | bytes accessed | tf_op | source)
XLA Modules:
  0.0 181.3 jit_solution(4194076185323199588)
XLA Ops:
  0.6 1.3 copy.7.order_ref
  2.0 168.2 %shard_map.68 = (f32[4,64,1024]{2,1,0:T(8,128)}, f32[4,2,4,64,1024]{4,3,2,1,0:T(8,128)}) custom-call(s32[4,1,2]{2,1,0:T(1,128)} %copy.7.order_ref, bf16[1024,2048]{1,0:T(8,128)(2,1)} %geno_hbm.1, f32[1024,256]{1,0:T(8,128)} %resid_hbm.1, bf16[2,1024,1024]{2,1,0:T(8,128)(2,1)} %inv_hbm.1, bf16[4,2048,256]{2,1,0:T(8,128)(2,1)} %noise_hbm.1), custom_call_target="tpu_custom_call" | custom-call | tf_op jit(solution)/shard_map/pallas_call | solution.py:318
  170.1 2.5 %copy.8 = f32[256,1024]{0,1:T(8,128)} copy(f32[256,1024]{1,0:T(8,128)} %bitcast.9) | data formatting | bytes 2097152 | tf_op jit(solution)/shard_map/reshape | solution.py:358
  172.7 8.7 %copy.9 = f32[4,2,1024,256]{3,2,1,0:T(8,128)} copy(f32[4,2,1024,256]{2,3,1,0:T(8,128)} %bitcast.7) | data formatting | bytes 16777216 | tf_op jit(solution)/shard_map/transpose | solution.py:359
where the time goes:
time: 182 us; the launch traced here: 181 us
  Pallas kernels  168 us (92%)
  local copies, waits for them, and re-layouts  12.5 us (7%)
    pallas_call x1, Pallas kernels, local(): pl.pallas_call(functools.partial(kernel, cfg), out_shape=(jax.ShapeDtypeS...  168 us
    transpose x1, local copies, waits for them, and re-layouts, local(): changes.reshape(stops, blocks, traits, block).transpose(0, 1, 3, 2)  8.67 us

commit v1 on v0

v1 whole, which is shorter than its diff:
```python
import functools

import jax
import jax.numpy as jnp
from jax import lax
from jax.experimental import pallas as pl
from jax.experimental.pallas import tpu as pltpu
from jax.sharding import PartitionSpec as P

epsilon = 1e-05
MESH = pl.DeviceIdType.MESH
CHUNKS = 4
PERIOD = 6
ORDER = (
    ("m", 3),
    ("c", 4),
    ("l", 5),
    ("d", 2),
    ("b", 3),
    ("a", 0),
    ("N", 0),
    ("c", 1),
    ("G", 1),
    ("d", 4),
    ("b", 0),
    ("V", 0),
)
LANES = 128
SUB = 8


def bits_of(n):
    steps = []
    s = 1
    while s < n:
        steps.append(s)
        s *= 2
    return steps


def kernel(
    cfg,
    order_ref,
    geno_hbm,
    resid_hbm,
    inv_hbm,
    noise_hbm,
    after_hbm,
    change_hbm,
    geno_ref,
    geno_t,
    resid_ref,
    inv_ref,
    inv_t,
    noise_raw,
    noise_ref,
    droot_ref,
    change_ref,
    ebuf,
    part,
    r1,
    rx,
    acc,
    full,
    meanp,
    stash,
    in_sem,
    out_sem,
    after_sem,
    p1s,
    p1r,
    xs,
    xr,
    fs,
    fr,
    zs,
    zr,
):
    n_ind, n_mark, n_chip, chunks, stops, count, block, levels = cfg
    tc = ebuf.shape[2]
    half = block // 2
    nb = half // LANES // levels
    seg_rows = nb * tc
    body_rows = levels * seg_rows
    groups = tc // SUB
    ind = lax.axis_index("ind")
    mark = lax.axis_index("mark")
    y = lax.axis_index("chip")
    core = lax.rem(ind, 2)
    x = lax.div(ind, 2)
    role = lax.rem(core + x + y, 2)
    other = 1 - role
    partner = {"ind": ind + 1 - 2 * core}
    nxt = {"mark": lax.rem(mark + 1, n_mark)}
    prv = {"mark": lax.rem(mark + n_mark - 1, n_mark)}

    def peer(axis, s):
        nx, ny = x, y
        if axis == "x":
            nx = x + s * (1 - 2 * lax.rem(lax.div(x, s), 2))
        else:
            ny = y + s * (1 - 2 * lax.rem(lax.div(y, s), 2))
        return {"ind": nx * 2 + lax.rem(role + nx + ny, 2), "chip": ny}

    peers = [peer("x", s) for s in bits_of(n_ind // 2)] + [peer("y", s) for s in bits_of(n_chip)]

    blocks = geno_ref.shape[0]
    per_visit = chunks // blocks
    piece = noise_ref.shape[3]
    loads = [pltpu.make_async_copy(resid_hbm, resid_ref, in_sem.at[0])]
    for k in range(blocks):
        loads.append(
            pltpu.make_async_copy(
                geno_hbm.at[:, k * block : (k + 1) * block], geno_ref.at[k], in_sem.at[1 + k]
            )
        )
    loads.append(pltpu.make_async_copy(noise_hbm, noise_raw, in_sem.at[1 + blocks]))
    loads.append(pltpu.make_async_copy(inv_hbm, inv_ref, in_sem.at[2 + blocks]))
    for load in loads:
        load.start()

    barrier = pltpu.get_barrier_semaphore()
    for dev in [partner, nxt, prv] + peers:
        pl.semaphore_signal(barrier, inc=1, device_id=dev, device_id_type=MESH)

    loads[0].wait()
    flipped = resid_ref[...].T
    for c in range(chunks):
        ebuf[0, c] = flipped[c * tc : (c + 1) * tc]
    for k in range(blocks):
        loads[1 + k].wait()
    pl.semaphore_wait(barrier, 3 + levels)

    def copy(src, dst, ssem, rsem, dev):
        return pltpu.make_async_remote_copy(
            src_ref=src, dst_ref=dst, send_sem=ssem, recv_sem=rsem, device_id=dev, device_id_type=MESH
        )

    def hop(stop, c):
        return copy(ebuf.at[stop, c], ebuf.at[stop + 1, c], zs.at[stop, c], zr.at[stop, c], nxt)

    def pair(c):
        return copy(part.at[c, other], r1.at[c], p1s.at[c], p1r.at[c], partner)

    def rows_of(g):
        return pl.ds(g * seg_rows, seg_rows + (SUB if g == levels - 1 else 0))

    def source(c, p):
        return part.at[c, role] if p == 0 else acc.at[c, p - 1]

    def swap(c, p, g):
        rows = rows_of(g)
        return copy(
            source(c, p).at[rows], rx.at[c, p, rows], xs.at[c, p, g], xr.at[c, p, g], peers[(g + p) % levels]
        )

    def forward(c):
        return copy(
            full.at[c, role, pl.ds(0, body_rows)],
            full.at[c, role, pl.ds(0, body_rows)],
            fs.at[c],
            fr.at[c],
            partner,
        )

    lane = lax.broadcasted_iota(jnp.int32, (SUB, LANES), 1)

    def bit(s):
        return lax.rem(lax.div(lane, s), 2) == 1

    def fold(tot):
        parts = [tot[SUB * g : SUB * (g + 1)] for g in range(groups)]
        s = LANES // 2
        while len(parts) > 1:
            take = bit(s)
            parts = [
                jnp.where(take, a + pltpu.roll(a, s, 1), b + pltpu.roll(b, LANES - s, 1))
                for a, b in zip(parts[::2], parts[1::2])
            ]
            s //= 2
        return parts[0]

    def unfold(tile):
        sums = []
        for g in range(groups):
            s, r, value = LANES // 2, g, tile
            for _ in bits_of(groups):
                value = jnp.where(bit(s) if r % 2 == 0 else jnp.logical_not(bit(s)), value, 0.0)
                s, r = s // 2, r // 2
            sums.append(jnp.sum(value, axis=1, keepdims=True))
        return jnp.concatenate(sums, axis=0)

    def put(c, h, s):
        for i in range(levels * nb):
            part[c, h, i * tc : (i + 1) * tc, :] = s[:, i * LANES : (i + 1) * LANES]

    def scaled_half(c, h):
        return jnp.concatenate(
            [(full[c, h, i * tc : (i + 1) * tc, :] * (1.0 / count)).astype(jnp.bfloat16) for i in range(levels * nb)],
            axis=1,
        )

    def span(h):
        return pl.ds(pl.multiple_of(h * half, half), half)

    def score(stop, j, c):
        k = order_ref[stop, 0, j]
        e = ebuf[stop, c]
        eb = e.astype(jnp.bfloat16)
        put(c, other, jnp.dot(eb, geno_ref[k, :, span(other)], preferred_element_type=jnp.float32))
        sq = e * e
        tot = sq[:, :LANES]
        for i in range(1, sq.shape[1] // LANES):
            tot = tot + sq[:, i * LANES : (i + 1) * LANES]
        tile = fold(tot)
        part[c, 0, body_rows:, :] = tile
        part[c, 1, body_rows:, :] = tile
        pair(c).start()
        put(c, role, jnp.dot(eb, geno_ref[k, :, span(role)], preferred_element_type=jnp.float32))

    def phase_a(stop, c):
        @pl.when(stop > 0)
        def _():
            hop(stop - 1, c).wait_recv()

        score(stop, 0, c)

    def phase_b(stop, c):
        pair(c).wait_recv()
        part[c, role] = part[c, role] + r1[c]
        for g in range(levels):
            swap(c, 0, g).start()

    def phase_c(stop, c):
        for p in range(levels - 1):
            for g in range(levels):
                swap(c, p, g).wait_recv()
            acc[c, p] = source(c, p)[...] + rx[c, p]
            for g in range(levels):
                swap(c, p + 1, g).start()
        pair(c).wait_send()

    def phase_d(stop, j, c):
        p = levels - 1
        for g in range(levels):
            swap(c, p, g).wait_recv()
        full[c, role] = source(c, p)[...] + rx[c, p]
        forward(c).start()
        k = order_ref[stop, 0, j]
        meanp[c] = jnp.dot(scaled_half(c, role), inv_t[k, span(role), :], preferred_element_type=jnp.float32)
        for p in range(levels):
            for g in range(levels):
                swap(c, p, g).wait_send()

    def phase_e(stop, j, c):
        k = order_ref[stop, 0, j]
        spread = unfold(full[c, role, body_rows:, :]) * (1.0 / count)
        root = jnp.sqrt((spread + epsilon) * (1.0 / count))
        noise = jnp.concatenate(
            [
                noise_ref[stop, j * per_visit + i, pl.ds(pl.multiple_of(c * tc, tc), tc), :]
                for i in range(per_visit)
            ],
            axis=1,
        ).astype(jnp.float32)
        forward(c).wait_recv()
        mean = meanp[c] + jnp.dot(
            scaled_half(c, other), inv_t[k, span(other), :], preferred_element_type=jnp.float32
        )
        change = mean + (root * droot_ref[k]) * noise
        stash[c, j] = change
        ebuf[stop, c] = ebuf[stop, c] - jnp.dot(
            change.astype(jnp.bfloat16), geno_t[k], preferred_element_type=jnp.float32
        )

    def at(x, fn):
        stop, c = lax.div(x, PERIOD), lax.rem(x, PERIOD)

        @pl.when((x >= 0) & (c < chunks) & (stop < stops))
        def _():
            fn(stop, c)

    def out_copy(stop, c):
        return pltpu.make_async_copy(change_ref.at[stop, :, c], change_hbm.at[stop, :, c], out_sem.at[stop, c])

    def last(stop, c):
        phase_e(stop, 1, c)
        hop(stop, c).start()
        forward(c).wait_send()
        first = order_ref[stop, 0, 0]
        change_ref[stop, 0, c] = stash[c, first]
        change_ref[stop, 1, c] = stash[c, 1 - first]
        out_copy(stop, c).start()

    def middle(stop, c):
        phase_e(stop, 0, c)
        score(stop, 1, c)
        forward(c).wait_send()

    def flip(stop, i):
        noise_ref[stop, i] = noise_raw[stop, pl.ds(pl.multiple_of(i * piece, piece), piece), :].T

    def turn(src, dst):
        for k in range(blocks):

            def one(i, z):
                cols = pl.ds(pl.multiple_of(i * LANES, LANES), LANES)
                dst[k, cols, :] = src[k, :, cols].T
                return z

            lax.fori_loop(0, block // LANES, one, 0)

    def prepare_noise():
        loads[1 + blocks].wait()
        lax.fori_loop(0, chunks, lambda i, x: (flip(0, i), x)[1], 0)

    def prepare_inverse():
        loads[2 + blocks].wait()
        turn(inv_ref, inv_t)
        eye = lax.broadcasted_iota(jnp.int32, (LANES, LANES), 0) == lax.broadcasted_iota(
            jnp.int32, (LANES, LANES), 1
        )
        for k in range(blocks):
            for i in range(0, block, LANES):
                tile = inv_ref[k, i : i + LANES, i : i + LANES].astype(jnp.float32)
                diag = jnp.sum(jnp.where(eye, tile, 0.0), axis=0, keepdims=True)
                droot_ref[k, :, i : i + LANES] = jnp.sqrt(diag)

    def prepare_genotypes():
        turn(geno_ref, geno_t)

    once = {"N": prepare_noise, "V": prepare_inverse, "G": prepare_genotypes}
    phases = {
        "a": phase_a,
        "b": phase_b,
        "c": phase_c,
        "m": middle,
        "l": last,
    }

    def body(t, carry):
        seen = 0
        for name, delay in ORDER:
            if name in once:
                pl.when(t == delay)(once[name])
            elif name == "d":
                visit = 0 if delay == min(d for n, d in ORDER if n == "d") else 1
                at(t - delay, lambda stop, c, visit=visit: phase_d(stop, visit, c))
            else:
                at(t - delay, phases[name])
        at(t + PERIOD, flip)
        return carry

    lax.fori_loop(0, PERIOD * (stops - 1) + chunks + max(delay for _, delay in ORDER), body, 0)

    def finish(c):
        return pltpu.make_async_copy(ebuf.at[stops, c], after_hbm.at[c], after_sem.at[c])

    for c in range(chunks):
        hop(stops - 1, c).wait_recv()
        finish(c).start()
    for c in range(chunks):
        for stop in range(stops):
            out_copy(stop, c).wait()
            hop(stop, c).wait_send()
        finish(c).wait()


def local(mesh_shape, genotypes, residual, posterior_inverse, gibbs_noise, visit_order):
    n_ind, n_mark, n_chip = mesh_shape
    levels = len(bits_of(n_ind // 2)) + len(bits_of(n_chip))
    people, traits = residual.shape
    count = people * n_ind * n_chip
    blocks, block = posterior_inverse.shape[:2]
    stops = gibbs_noise.shape[0]
    chunks = CHUNKS
    tc = traits // chunks
    rows = block // 2 // LANES * tc + SUB
    f32, bf16 = jnp.float32, jnp.bfloat16
    cfg = (n_ind, n_mark, n_chip, chunks, stops, count, block, levels)
    hbm = pl.BlockSpec(memory_space=pl.ANY)
    dma = pltpu.SemaphoreType.DMA
    after, changes = pl.pallas_call(
        functools.partial(kernel, cfg),
        out_shape=(
            jax.ShapeDtypeStruct((chunks, tc, people), f32),
            jax.ShapeDtypeStruct((stops, blocks, chunks, tc, block), f32),
        ),
        in_specs=[pl.BlockSpec(memory_space=pltpu.SMEM)] + [hbm] * 4,
        out_specs=(hbm, hbm),
        scratch_shapes=[
            pltpu.VMEM((blocks, people, block), bf16),
            pltpu.VMEM((blocks, block, people), bf16),
            pltpu.VMEM((people, traits), f32),
            pltpu.VMEM((blocks, block, block), bf16),
            pltpu.VMEM((blocks, block, block), bf16),
            pltpu.VMEM((stops, blocks * block, traits), bf16),
            pltpu.VMEM((stops, chunks, traits, blocks * block // chunks), bf16),
            pltpu.VMEM((blocks, 1, block), f32),
            pltpu.VMEM((stops, blocks, chunks, tc, block), f32),
            pltpu.VMEM((stops + 1, chunks, tc, people), f32),
            pltpu.VMEM((chunks, 2, rows, LANES), f32),
            pltpu.VMEM((chunks, rows, LANES), f32),
            pltpu.VMEM((chunks, levels, rows, LANES), f32),
            pltpu.VMEM((chunks, levels - 1, rows, LANES), f32),
            pltpu.VMEM((chunks, 2, rows, LANES), f32),
            pltpu.VMEM((chunks, tc, block), f32),
            pltpu.VMEM((chunks, blocks, tc, block), f32),
            dma((3 + blocks,)),
            dma((stops, chunks)),
            dma((chunks,)),
            dma((chunks,)),
            dma((chunks,)),
            dma((chunks, levels, levels)),
            dma((chunks, levels, levels)),
            dma((chunks,)),
            dma((chunks,)),
            dma((stops, chunks)),
            dma((stops, chunks)),
        ],
        compiler_params=pltpu.CompilerParams(
            collective_id=0, has_side_effects=True, vmem_limit_bytes=60 * 1024 * 1024
        ),
    )(visit_order, genotypes, residual, posterior_inverse, gibbs_noise)
    after = after.reshape(traits, people).T
    changes = changes.reshape(stops, blocks, traits, block).transpose(0, 1, 3, 2)
    return after, changes.reshape(stops, blocks * block, traits)


def solution(mesh):
    in_specs = (
        P(("ind", "chip"), "mark"),
        P(("ind", "chip"), "mark"),
        P("mark", None, None),
        P(None, "mark", None),
        P(None, "mark", None),
    )
    out_specs = (P(("ind", "chip"), "mark"), P(None, "mark", None))
    shape = (mesh.shape["ind"], mesh.shape["mark"], mesh.shape["chip"])
    return jax.shard_map(
        functools.partial(local, shape), mesh=mesh, in_specs=in_specs, out_specs=out_specs, check_vma=False
    )
```

time: 182 us -> 175 us (0.962)
  Pallas kernels: 168 us -> 161 us
    pallas_call x1, Pallas kernels: 168 us -> 161 us  [local(): pl.pallas_call(functools.partial(kernel, cfg), out_shape=(jax.ShapeDtypeS...]
where the time goes in v1:
time: 175 us
  Pallas kernels  161 us (92%)
  local copies, waits for them, and re-layouts  12.5 us (7%)
    pallas_call x1, Pallas kernels, local(): pl.pallas_call(functools.partial(kernel, cfg), out_shape=(jax.ShapeDtypeS...  161 us
    transpose x1, local copies, waits for them, and re-layouts, local(): changes.reshape(stops, blocks, traits, block).transpose(0, 1, 3, 2)  8.67 us

profile of v1, /device:TPU:0, one launch (start us, length us, event | category | flops | bytes accessed | tf_op | source)
XLA Modules:
  0.0 174.6 jit_solution(7055067075862275401)
XLA Ops:
  0.6 1.3 copy.7.order_ref
  2.0 161.4 %shard_map.68 = (f32[4,64,1024]{2,1,0:T(8,128)}, f32[4,2,4,64,1024]{4,3,2,1,0:T(8,128)}) custom-call(s32[4,1,2]{2,1,0:T(1,128)} %copy.7.order_ref, bf16[1024,2048]{1,0:T(8,128)(2,1)} %geno_hbm.1, f32[1024,256]{1,0:T(8,128)} %resid_hbm.1, bf16[2,1024,1024]{2,1,0:T(8,128)(2,1)} %inv_hbm.1, bf16[4,2048,256]{2,1,0:T(8,128)(2,1)} %noise_hbm.1), custom_call_target="tpu_custom_call" | custom-call | tf_op jit(solution)/shard_map/pallas_call | solution.py:383
  163.4 2.5 %copy.8 = f32[256,1024]{0,1:T(8,128)} copy(f32[256,1024]{1,0:T(8,128)} %bitcast.9) | data formatting | bytes 2097152 | tf_op jit(solution)/shard_map/reshape | solution.py:425
  165.9 8.7 %copy.9 = f32[4,2,1024,256]{3,2,1,0:T(8,128)} copy(f32[4,2,1024,256]{2,3,1,0:T(8,128)} %bitcast.7) | data formatting | bytes 16777216 | tf_op jit(solution)/shard_map/transpose | solution.py:426

commit v2 on v1

--- a/solution.py
+++ b/solution.py
@@ -10,20 +10,20 @@
 epsilon = 1e-05
 MESH = pl.DeviceIdType.MESH
 CHUNKS = 4
-PERIOD = 6
+PERIOD = 5
 ORDER = (
-    ("m", 3),
-    ("c", 4),
-    ("l", 5),
-    ("d", 2),
-    ("b", 3),
+    ("G", 1),
+    ("m", 2),
+    ("c", 1),
     ("a", 0),
     ("N", 0),
-    ("c", 1),
-    ("G", 1),
-    ("d", 4),
+    ("b", 2),
     ("b", 0),
-    ("V", 0),
+    ("e", 3),
+    ("V", 1),
+    ("d", 1),
+    ("l", 3),
+    ("c", 2),
 )
 LANES = 128
 SUB = 8
@@ -334,18 +334,16 @@
         "a": phase_a,
         "b": phase_b,
         "c": phase_c,
+        "d": lambda stop, c: phase_d(stop, 0, c),
+        "e": lambda stop, c: phase_d(stop, 1, c),
         "m": middle,
         "l": last,
     }
 
     def body(t, carry):
-        seen = 0
         for name, delay in ORDER:
             if name in once:
                 pl.when(t == delay)(once[name])
-            elif name == "d":
-                visit = 0 if delay == min(d for n, d in ORDER if n == "d") else 1
-                at(t - delay, lambda stop, c, visit=visit: phase_d(stop, visit, c))
             else:
                 at(t - delay, phases[name])
         at(t + PERIOD, flip)

time: 175 us -> 166 us (0.949)
  Pallas kernels: 161 us -> 152 us
    pallas_call x1, Pallas kernels: 161 us -> 152 us  [local(): pl.pallas_call(functools.partial(kernel, cfg), out_shape=(jax.ShapeDtypeS...]
where the time goes in v2:
time: 166 us
  Pallas kernels  152 us (92%)
  local copies, waits for them, and re-layouts  12.5 us (8%)
    pallas_call x1, Pallas kernels, local(): pl.pallas_call(functools.partial(kernel, cfg), out_shape=(jax.ShapeDtypeS...  152 us
    transpose x1, local copies, waits for them, and re-layouts, local(): changes.reshape(stops, blocks, traits, block).transpose(0, 1, 3, 2)  8.67 us

profile of v2, /device:TPU:0, one launch (start us, length us, event | category | flops | bytes accessed | tf_op | source)
XLA Modules:
  0.0 165.7 jit_solution(4816786050789119241)
XLA Ops:
  0.6 1.3 copy.7.order_ref
  2.0 152.5 %shard_map.68 = (f32[4,64,1024]{2,1,0:T(8,128)}, f32[4,2,4,64,1024]{4,3,2,1,0:T(8,128)}) custom-call(s32[4,1,2]{2,1,0:T(1,128)} %copy.7.order_ref, bf16[1024,2048]{1,0:T(8,128)(2,1)} %geno_hbm.1, f32[1024,256]{1,0:T(8,128)} %resid_hbm.1, bf16[2,1024,1024]{2,1,0:T(8,128)(2,1)} %inv_hbm.1, bf16[4,2048,256]{2,1,0:T(8,128)(2,1)} %noise_hbm.1), custom_call_target="tpu_custom_call" | custom-call | tf_op jit(solution)/shard_map/pallas_call | solution.py:381
  154.5 2.5 %copy.8 = f32[256,1024]{0,1:T(8,128)} copy(f32[256,1024]{1,0:T(8,128)} %bitcast.9) | data formatting | bytes 2097152 | tf_op jit(solution)/shard_map/reshape | solution.py:423
  157.0 8.7 %copy.9 = f32[4,2,1024,256]{3,2,1,0:T(8,128)} copy(f32[4,2,1024,256]{2,3,1,0:T(8,128)} %bitcast.7) | data formatting | bytes 16777216 | tf_op jit(solution)/shard_map/transpose | solution.py:424

commit v3 on v2

--- a/solution.py
+++ b/solution.py
@@ -9,21 +9,21 @@
 
 epsilon = 1e-05
 MESH = pl.DeviceIdType.MESH
-CHUNKS = 4
-PERIOD = 5
+CHUNKS = 8
+PERIOD = 10
 ORDER = (
-    ("G", 1),
-    ("m", 2),
-    ("c", 1),
+    ("c", 2),
     ("a", 0),
     ("N", 0),
-    ("b", 2),
+    ("V", 2),
+    ("d", 3),
+    ("b", 4),
+    ("l", 7),
+    ("c", 5),
+    ("G", 1),
     ("b", 0),
-    ("e", 3),
-    ("V", 1),
-    ("d", 1),
-    ("l", 3),
-    ("c", 2),
+    ("m", 3),
+    ("e", 6),
 )
 LANES = 128
 SUB = 8

time: 166 us -> 163 us (0.982)
  Pallas kernels: 152 us -> 149 us
    pallas_call x1, Pallas kernels: 152 us -> 149 us  [local(): pl.pallas_call(functools.partial(kernel, cfg), out_shape=(jax.ShapeDtypeS...]
where the time goes in v3:
time: 163 us; the launch traced here: 162 us
  Pallas kernels  149 us (91%)
  local copies, waits for them, and re-layouts  12.5 us (8%)
    pallas_call x1, Pallas kernels, local(): pl.pallas_call(functools.partial(kernel, cfg), out_shape=(jax.ShapeDtypeS...  149 us
    transpose x1, local copies, waits for them, and re-layouts, local(): changes.reshape(stops, blocks, traits, block).transpose(0, 1, 3, 2)  8.67 us

profile of v3, /device:TPU:0, one launch (start us, length us, event | category | flops | bytes accessed | tf_op | source)
XLA Modules:
  0.0 162.4 jit_solution(3391523306045329592)
XLA Ops:
  0.6 1.3 copy.7.order_ref
  2.0 149.2 %shard_map.68 = (f32[8,32,1024]{2,1,0:T(8,128)}, f32[4,2,8,32,1024]{4,3,2,1,0:T(8,128)}) custom-call(s32[4,1,2]{2,1,0:T(1,128)} %copy.7.order_ref, bf16[1024,2048]{1,0:T(8,128)(2,1)} %geno_hbm.1, f32[1024,256]{1,0:T(8,128)} %resid_hbm.1, bf16[2,1024,1024]{2,1,0:T(8,128)(2,1)} %inv_hbm.1, bf16[4,2048,256]{2,1,0:T(8,128)(2,1)} %noise_hbm.1), custom_call_target="tpu_custom_call" | custom-call | tf_op jit(solution)/shard_map/pallas_call | solution.py:381
  151.2 2.5 %copy.8 = f32[256,1024]{0,1:T(8,128)} copy(f32[256,1024]{1,0:T(8,128)} %bitcast.9) | data formatting | bytes 2097152 | tf_op jit(solution)/shard_map/reshape | solution.py:423
  153.7 8.7 %copy.9 = f32[4,2,1024,256]{3,2,1,0:T(8,128)} copy(f32[4,2,1024,256]{2,3,1,0:T(8,128)} %bitcast.7) | data formatting | bytes 16777216 | tf_op jit(solution)/shard_map/transpose | solution.py:424
